TPU v7x, 32 devices: a whole 2x2x4 slice. The times are simulated.
32 devices in a mesh: shell: 4 (over x, core), sky: 8 (over z, y).
Axes of the slice: x: 2, y: 2, z: 4, core: 2. Of those that a mesh axis runs over, the one named last changes fastest.
Arguments:
- coords: int32 [3, 4, 8, 512], P(None, 'shell', 'sky'), may hold values from 0 to 2047, as said below
- weights: bfloat16 [4, 8, 512], P('shell', 'sky'), may hold values from 0.5 to 2
- live: int32 [4, 8], P('shell', 'sky'), may hold values from 128 to 512, as said below
Outputs:
- jackknife: float32 [4, 64, 600], P('shell', 'sky')
Inputs may be any that keep to these rules, and one draw needn't show every extreme that they name: On device (a, b), coords[0] lies in [a * 256, (a+1) * 256), coords[1] in [b * 256, (b+1) * 256), coords[2] in [0, 1024). `live`: live slots are the first ones of a device; some device is full in every draw.
All inputs are finite; a program needn't handle non-finite values.
Results may differ from a plain program's by a relative error of at most 0.0003.
Values sent between devices are 32-bit elements; how exact they have to be, the bound alone decides.
A program may use at most 64 MiB of HBM per device.

v0:
```python
import math
import jax
import jax.numpy as jnp
from jax import lax
from jax.sharding import PartitionSpec as P

PART_DEV = 512
SIDE_CELLS = 256
SPAN_CELLS = 1024
SUBREGIONS = 8
S_BINS = 30
MU_BINS = 20


def padded(block, sides, width):
    for axis, dim in sides:
        count = lax.axis_size(axis)
        forward = [(i, i + 1) for i in range(count - 1)]
        backward = [(target, source) for source, target in forward]
        low = lax.ppermute(
            lax.slice_in_dim(block, block.shape[dim] - width, None, axis=dim), axis, forward
        )
        high = lax.ppermute(lax.slice_in_dim(block, 0, width, axis=dim), axis, backward)
        block = jnp.concatenate([low, block, high], axis=dim)
    return block


def edge_values():
    return [int(4.0 * 10.0 ** (4.0 * level / S_BINS) + 0.5) for level in range(S_BINS + 1)]


def bin_scale(patches):
    edges = edge_values()
    factor = SIDE_CELLS * SIDE_CELLS * SPAN_CELLS / (patches * PART_DEV * PART_DEV)
    values = []
    for level in range(S_BINS):
        volume = 4.0 * math.pi / 3.0 * (edges[level + 1] ** 1.5 - edges[level] ** 1.5) / MU_BINS
        values = values + [factor / volume] * MU_BINS
    return jnp.asarray(values, dtype=jnp.float32)


def pair_block(own_pos, far_pos, far_weight):
    edges = edge_values()
    radial_gap = jnp.minimum(jnp.abs(own_pos[0][:, None] - far_pos[0][None, :]), 255)
    across_gap = jnp.minimum(jnp.abs(own_pos[1][:, None] - far_pos[1][None, :]), 255)
    depth_gap = jnp.minimum(jnp.abs(own_pos[2][:, None] - far_pos[2][None, :]), 255)
    squared = radial_gap * radial_gap + across_gap * across_gap + depth_gap * depth_gap
    radial_sq = radial_gap * radial_gap * (MU_BINS * MU_BINS)
    s_index = jnp.zeros_like(squared)
    for level in range(1, S_BINS):
        s_index = s_index + (squared >= edges[level]).astype(jnp.int32)
    mu_index = jnp.zeros_like(squared)
    for level in range(1, MU_BINS):
        mu_index = mu_index + (radial_sq >= level * level * squared).astype(jnp.int32)
    inside = (squared >= edges[0]) & (squared < edges[S_BINS])
    s_levels = lax.iota(jnp.int32, S_BINS)
    mu_levels = lax.iota(jnp.int32, MU_BINS)
    s_hot = ((s_index[:, :, None] == s_levels[None, None, :]) & inside[:, :, None]).astype(
        jnp.float32
    )
    s_weighted = (s_hot * far_weight[None, :, None]).astype(jnp.bfloat16)
    mu_hot = (mu_index[:, :, None] == mu_levels[None, None, :]).astype(jnp.bfloat16)
    return jnp.einsum("ijs,ijm->ism", s_weighted, mu_hot, preferred_element_type=jnp.float32)


def local(coords, weights, live):
    live_count = live[0, 0]
    parts = coords.shape[3]
    slots = lax.iota(jnp.int32, parts)
    own_weight = jnp.where(slots < live_count, weights[0, 0].astype(jnp.float32), 0.0)
    own_pos = coords.reshape(3, parts)
    packed = jnp.concatenate(
        [coords.astype(jnp.float32), own_weight.reshape(1, 1, 1, parts)], axis=0
    )
    tile_rows = min(256, parts)
    tiles_live = (live_count + tile_rows - 1) // tile_rows
    empty = jnp.zeros((SUBREGIONS, S_BINS, MU_BINS), jnp.float32)
    region_levels = lax.iota(jnp.int32, SUBREGIONS)
    result = padded(packed, (("shell", 1), ("sky", 2)), 1)
    far_pos = result[:3].reshape(3, 9 * parts).astype(jnp.int32)
    far_weight = result[3].reshape(9 * parts)
    blocks = far_pos.shape[1] // parts

    def add_tile(index, running):
        start = index * tile_rows
        rows_pos = lax.dynamic_slice_in_dim(own_pos, start, tile_rows, 1)
        rows_weight = lax.dynamic_slice_in_dim(own_weight, start, tile_rows, 0)

        def add_block(block, per_row):
            offset = block * parts
            block_pos = lax.dynamic_slice_in_dim(far_pos, offset, parts, 1)
            block_weight = lax.dynamic_slice_in_dim(far_weight, offset, parts, 0)
            return per_row + pair_block(rows_pos, block_pos, block_weight)

        per_row = lax.fori_loop(
            0, blocks, add_block, jnp.zeros((tile_rows, S_BINS, MU_BINS), jnp.float32)
        )
        region = rows_pos[2] // (SPAN_CELLS // SUBREGIONS)
        region_weight = jnp.where(
            region[:, None] == region_levels[None, :], rows_weight[:, None], 0.0
        )
        folded = jnp.sum(region_weight[:, :, None, None] * per_row[:, None, :, :], axis=0)
        return running + folded

    histogram = lax.fori_loop(0, tiles_live, add_tile, empty)
    by_region = histogram.reshape(SUBREGIONS, S_BINS * MU_BINS)
    shell_total = lax.psum(jnp.sum(by_region, axis=0), "sky")
    scale = bin_scale(lax.axis_size("sky"))
    leave = (shell_total[None, :] - by_region) * scale[None, :]
    return leave.reshape(1, SUBREGIONS, S_BINS * MU_BINS)


def solution(mesh):
    in_specs = (P(None, "shell", "sky", None), P("shell", "sky", None), P("shell", "sky"))
    out_specs = P("shell", "sky", None)
    return jax.shard_map(local, mesh=mesh, in_specs=in_specs, out_specs=out_specs, check_vma=False)
```

profile of v0, /device:TPU:2, one launch (start us, length us, event | category | flops | bytes accessed | tf_op | source)
XLA Modules:
  0.0 244.2 jit_solution(1972182534379924726)
XLA Ops:
  4.0 2.4 collective-permute-start
  10.3 4.5 %collective-permute-start.2 = (f32[4,3,1,512]{3,2,1,0:T(1,128)S(1)}, f32[4,3,1,512]{3,2,1,0:T(1,128)S(1)}, u32[]{:S(2)}, u32[]{:S(2)}) collective-permute-start(f32[4,3,1,512]{3,2,1,0:T(1,128)S(1)} %pad_maximum_fusion.2), channel_id=1, source_target_pairs={{0,1},{1,2},{2,3},{3,4},{4,5},{5,6},{6,7},{8,9},{9,10},{10,11},{11... | collective-permute-start | bytes 73736 | tf_op jit(solution)/shard_map/ppermute | solution.py:20
  16.6 101.9 %while.36 = (s32[]{:T(128)}, f32[8,30,20]{0,2,1:T(8,128)S(1)}, s32[]{:T(128)}, s32[3,512]{1,0:T(4,128)S(1)}, f32[512]{0:T(512)S(1)}, /*index=5*/s32[3,4608]{1,0:...) while((s32[]{:T(128)}, f32[8,30,20]{0,2,1:T(8,128)S(1)}, ...), condition=%wide.region_4.5_spmd.clone, body=%wide.region_0.4_spmd.clone.sunk | while | flops 199642880 | bytes 5579304 | solution.py:105
  16.6 98.5 %while.37 = (s32[]{:T(128)}, f32[256,30,20]{1,2,0:T(8,128)}, s32[3,256]{1,0:T(4,128)S(1)}, s32[3,4608]{1,0:T(4,128)S(1)}, bf16[4608]{0:T(1024)(128)(2,1)S(1)}, /...) while((s32[]{:T(128)}, f32[256,30,20]{1,2,0:T(8,128)}, ...), condition=%wide.region_2.2_spmd.clone, body=%wide.region_1.1_spmd.clone.sunk | while | flops 197177344 | bytes 3628245 | solution.py:95
  16.8 3.3 %convert_add_fusion.3 = (s32[256,512]{1,0:T(8,128)S(1)}, s32[256,512]{1,0:T(8,128)S(1)}) fusion(s32[512]{0:T(512)S(1)} %bitcast.35, s32[256]{0:T(256)S(1)} %bitcast.39, s32[512]{0:T(512)S(1)} %bitcast.31, s32[256]{0:T(256)S(1)} %bitcast.37, s32[512]{0:T(512)S(1)} %bitcast.33, s32[256]{0:T(256)S(1)} %bitcast.41), kind=kLoop, calls=%fused_computation.31.clone.1 | loop fusion | flops 22937600 | bytes 1057792 | tf_op jit(solution)/shard_map/while/body/while/body/eval_jaxpr/add | solution.py:51
  20.7 5.7 %select_add_fusion.2 = f32[256,30,20]{1,2,0:T(8,128)} fusion(f32[256,30,20]{1,2,0:T(8,128)} %get-tuple-element.400, s32[256,512]{1,0:T(8,128)S(1)} %get-tuple-element.386, bf16[512]{0:T(512)(128)(2,1)S(1)} %dynamic_slice.36, s32[256,512]{1,0:T(8,128)S(1)} %get-tuple-element.387, pred[256,512]{1,0:T(8,128)(4,1)S(1)} %compare_and_fusion.2, ...), kind=kOutput, calls=%fused_computation.11.clone.1 | convolution fusion | flops 172011520 | bytes 2409473 | tf_op jit(solution)/shard_map/while/body/while/body/eval_jaxpr/ijs,ijm->ism/dot_general | solution.py:63
  26.5 3.3 %convert_add_fusion.3 = (s32[256,512]{1,0:T(8,128)S(1)}, s32[256,512]{1,0:T(8,128)S(1)}) fusion(s32[512]{0:T(512)S(1)} %bitcast.35, s32[256]{0:T(256)S(1)} %bitcast.39, s32[512]{0:T(512)S(1)} %bitcast.31, s32[256]{0:T(256)S(1)} %bitcast.37, s32[512]{0:T(512)S(1)} %bitcast.33, s32[256]{0:T(256)S(1)} %bitcast.41), kind=kLoop, calls=%fused_computation.31.clone.1 | loop fusion | flops 22937600 | bytes 1057792 | tf_op jit(solution)/shard_map/while/body/while/body/eval_jaxpr/add | solution.py:51
  30.4 7.1 %select_add_fusion.2 = f32[256,30,20]{1,2,0:T(8,128)} fusion(f32[256,30,20]{1,2,0:T(8,128)} %get-tuple-element.400, s32[256,512]{1,0:T(8,128)S(1)} %get-tuple-element.386, bf16[512]{0:T(512)(128)(2,1)S(1)} %dynamic_slice.36, s32[256,512]{1,0:T(8,128)S(1)} %get-tuple-element.387, pred[256,512]{1,0:T(8,128)(4,1)S(1)} %compare_and_fusion.2, ...), kind=kOutput, calls=%fused_computation.11.clone.1 | convolution fusion | flops 172011520 | bytes 2409473 | tf_op jit(solution)/shard_map/while/body/while/body/eval_jaxpr/ijs,ijm->ism/dot_general | solution.py:63
  37.6 3.3 %convert_add_fusion.3 = (s32[256,512]{1,0:T(8,128)S(1)}, s32[256,512]{1,0:T(8,128)S(1)}) fusion(s32[512]{0:T(512)S(1)} %bitcast.35, s32[256]{0:T(256)S(1)} %bitcast.39, s32[512]{0:T(512)S(1)} %bitcast.31, s32[256]{0:T(256)S(1)} %bitcast.37, s32[512]{0:T(512)S(1)} %bitcast.33, s32[256]{0:T(256)S(1)} %bitcast.41), kind=kLoop, calls=%fused_computation.31.clone.1 | loop fusion | flops 22937600 | bytes 1057792 | tf_op jit(solution)/shard_map/while/body/while/body/eval_jaxpr/add | solution.py:51
  41.5 7.1 %select_add_fusion.2 = f32[256,30,20]{1,2,0:T(8,128)} fusion(f32[256,30,20]{1,2,0:T(8,128)} %get-tuple-element.400, s32[256,512]{1,0:T(8,128)S(1)} %get-tuple-element.386, bf16[512]{0:T(512)(128)(2,1)S(1)} %dynamic_slice.36, s32[256,512]{1,0:T(8,128)S(1)} %get-tuple-element.387, pred[256,512]{1,0:T(8,128)(4,1)S(1)} %compare_and_fusion.2, ...), kind=kOutput, calls=%fused_computation.11.clone.1 | convolution fusion | flops 172011520 | bytes 2409473 | tf_op jit(solution)/shard_map/while/body/while/body/eval_jaxpr/ijs,ijm->ism/dot_general | solution.py:63
  48.7 3.3 %convert_add_fusion.3 = (s32[256,512]{1,0:T(8,128)S(1)}, s32[256,512]{1,0:T(8,128)S(1)}) fusion(s32[512]{0:T(512)S(1)} %bitcast.35, s32[256]{0:T(256)S(1)} %bitcast.39, s32[512]{0:T(512)S(1)} %bitcast.31, s32[256]{0:T(256)S(1)} %bitcast.37, s32[512]{0:T(512)S(1)} %bitcast.33, s32[256]{0:T(256)S(1)} %bitcast.41), kind=kLoop, calls=%fused_computation.31.clone.1 | loop fusion | flops 22937600 | bytes 1057792 | tf_op jit(solution)/shard_map/while/body/while/body/eval_jaxpr/add | solution.py:51
  52.6 7.1 %select_add_fusion.2 = f32[256,30,20]{1,2,0:T(8,128)} fusion(f32[256,30,20]{1,2,0:T(8,128)} %get-tuple-element.400, s32[256,512]{1,0:T(8,128)S(1)} %get-tuple-element.386, bf16[512]{0:T(512)(128)(2,1)S(1)} %dynamic_slice.36, s32[256,512]{1,0:T(8,128)S(1)} %get-tuple-element.387, pred[256,512]{1,0:T(8,128)(4,1)S(1)} %compare_and_fusion.2, ...), kind=kOutput, calls=%fused_computation.11.clone.1 | convolution fusion | flops 172011520 | bytes 2409473 | tf_op jit(solution)/shard_map/while/body/while/body/eval_jaxpr/ijs,ijm->ism/dot_general | solution.py:63
  59.8 3.3 %convert_add_fusion.3 = (s32[256,512]{1,0:T(8,128)S(1)}, s32[256,512]{1,0:T(8,128)S(1)}) fusion(s32[512]{0:T(512)S(1)} %bitcast.35, s32[256]{0:T(256)S(1)} %bitcast.39, s32[512]{0:T(512)S(1)} %bitcast.31, s32[256]{0:T(256)S(1)} %bitcast.37, s32[512]{0:T(512)S(1)} %bitcast.33, s32[256]{0:T(256)S(1)} %bitcast.41), kind=kLoop, calls=%fused_computation.31.clone.1 | loop fusion | flops 22937600 | bytes 1057792 | tf_op jit(solution)/shard_map/while/body/while/body/eval_jaxpr/add | solution.py:51
  63.7 7.1 %select_add_fusion.2 = f32[256,30,20]{1,2,0:T(8,128)} fusion(f32[256,30,20]{1,2,0:T(8,128)} %get-tuple-element.400, s32[256,512]{1,0:T(8,128)S(1)} %get-tuple-element.386, bf16[512]{0:T(512)(128)(2,1)S(1)} %dynamic_slice.36, s32[256,512]{1,0:T(8,128)S(1)} %get-tuple-element.387, pred[256,512]{1,0:T(8,128)(4,1)S(1)} %compare_and_fusion.2, ...), kind=kOutput, calls=%fused_computation.11.clone.1 | convolution fusion | flops 172011520 | bytes 2409473 | tf_op jit(solution)/shard_map/while/body/while/body/eval_jaxpr/ijs,ijm->ism/dot_general | solution.py:63
  70.8 3.3 %convert_add_fusion.3 = (s32[256,512]{1,0:T(8,128)S(1)}, s32[256,512]{1,0:T(8,128)S(1)}) fusion(s32[512]{0:T(512)S(1)} %bitcast.35, s32[256]{0:T(256)S(1)} %bitcast.39, s32[512]{0:T(512)S(1)} %bitcast.31, s32[256]{0:T(256)S(1)} %bitcast.37, s32[512]{0:T(512)S(1)} %bitcast.33, s32[256]{0:T(256)S(1)} %bitcast.41), kind=kLoop, calls=%fused_computation.31.clone.1 | loop fusion | flops 22937600 | bytes 1057792 | tf_op jit(solution)/shard_map/while/body/while/body/eval_jaxpr/add | solution.py:51
  74.8 7.1 %select_add_fusion.2 = f32[256,30,20]{1,2,0:T(8,128)} fusion(f32[256,30,20]{1,2,0:T(8,128)} %get-tuple-element.400, s32[256,512]{1,0:T(8,128)S(1)} %get-tuple-element.386, bf16[512]{0:T(512)(128)(2,1)S(1)} %dynamic_slice.36, s32[256,512]{1,0:T(8,128)S(1)} %get-tuple-element.387, pred[256,512]{1,0:T(8,128)(4,1)S(1)} %compare_and_fusion.2, ...), kind=kOutput, calls=%fused_computation.11.clone.1 | convolution fusion | flops 172011520 | bytes 2409473 | tf_op jit(solution)/shard_map/while/body/while/body/eval_jaxpr/ijs,ijm->ism/dot_general | solution.py:63
  81.9 3.3 %convert_add_fusion.3 = (s32[256,512]{1,0:T(8,128)S(1)}, s32[256,512]{1,0:T(8,128)S(1)}) fusion(s32[512]{0:T(512)S(1)} %bitcast.35, s32[256]{0:T(256)S(1)} %bitcast.39, s32[512]{0:T(512)S(1)} %bitcast.31, s32[256]{0:T(256)S(1)} %bitcast.37, s32[512]{0:T(512)S(1)} %bitcast.33, s32[256]{0:T(256)S(1)} %bitcast.41), kind=kLoop, calls=%fused_computation.31.clone.1 | loop fusion | flops 22937600 | bytes 1057792 | tf_op jit(solution)/shard_map/while/body/while/body/eval_jaxpr/add | solution.py:51
  85.9 7.1 %select_add_fusion.2 = f32[256,30,20]{1,2,0:T(8,128)} fusion(f32[256,30,20]{1,2,0:T(8,128)} %get-tuple-element.400, s32[256,512]{1,0:T(8,128)S(1)} %get-tuple-element.386, bf16[512]{0:T(512)(128)(2,1)S(1)} %dynamic_slice.36, s32[256,512]{1,0:T(8,128)S(1)} %get-tuple-element.387, pred[256,512]{1,0:T(8,128)(4,1)S(1)} %compare_and_fusion.2, ...), kind=kOutput, calls=%fused_computation.11.clone.1 | convolution fusion | flops 172011520 | bytes 2409473 | tf_op jit(solution)/shard_map/while/body/while/body/eval_jaxpr/ijs,ijm->ism/dot_general | solution.py:63
  93.0 3.3 %convert_add_fusion.3 = (s32[256,512]{1,0:T(8,128)S(1)}, s32[256,512]{1,0:T(8,128)S(1)}) fusion(s32[512]{0:T(512)S(1)} %bitcast.35, s32[256]{0:T(256)S(1)} %bitcast.39, s32[512]{0:T(512)S(1)} %bitcast.31, s32[256]{0:T(256)S(1)} %bitcast.37, s32[512]{0:T(512)S(1)} %bitcast.33, s32[256]{0:T(256)S(1)} %bitcast.41), kind=kLoop, calls=%fused_computation.31.clone.1 | loop fusion | flops 22937600 | bytes 1057792 | tf_op jit(solution)/shard_map/while/body/while/body/eval_jaxpr/add | solution.py:51
  96.9 7.1 %select_add_fusion.2 = f32[256,30,20]{1,2,0:T(8,128)} fusion(f32[256,30,20]{1,2,0:T(8,128)} %get-tuple-element.400, s32[256,512]{1,0:T(8,128)S(1)} %get-tuple-element.386, bf16[512]{0:T(512)(128)(2,1)S(1)} %dynamic_slice.36, s32[256,512]{1,0:T(8,128)S(1)} %get-tuple-element.387, pred[256,512]{1,0:T(8,128)(4,1)S(1)} %compare_and_fusion.2, ...), kind=kOutput, calls=%fused_computation.11.clone.1 | convolution fusion | flops 172011520 | bytes 2409473 | tf_op jit(solution)/shard_map/while/body/while/body/eval_jaxpr/ijs,ijm->ism/dot_general | solution.py:63
  104.1 3.3 %convert_add_fusion.3 = (s32[256,512]{1,0:T(8,128)S(1)}, s32[256,512]{1,0:T(8,128)S(1)}) fusion(s32[512]{0:T(512)S(1)} %bitcast.35, s32[256]{0:T(256)S(1)} %bitcast.39, s32[512]{0:T(512)S(1)} %bitcast.31, s32[256]{0:T(256)S(1)} %bitcast.37, s32[512]{0:T(512)S(1)} %bitcast.33, s32[256]{0:T(256)S(1)} %bitcast.41), kind=kLoop, calls=%fused_computation.31.clone.1 | loop fusion | flops 22937600 | bytes 1057792 | tf_op jit(solution)/shard_map/while/body/while/body/eval_jaxpr/add | solution.py:51
  108.0 7.1 %select_add_fusion.2 = f32[256,30,20]{1,2,0:T(8,128)} fusion(f32[256,30,20]{1,2,0:T(8,128)} %get-tuple-element.400, s32[256,512]{1,0:T(8,128)S(1)} %get-tuple-element.386, bf16[512]{0:T(512)(128)(2,1)S(1)} %dynamic_slice.36, s32[256,512]{1,0:T(8,128)S(1)} %get-tuple-element.387, pred[256,512]{1,0:T(8,128)(4,1)S(1)} %compare_and_fusion.2, ...), kind=kOutput, calls=%fused_computation.11.clone.1 | convolution fusion | flops 172011520 | bytes 2409473 | tf_op jit(solution)/shard_map/while/body/while/body/eval_jaxpr/ijs,ijm->ism/dot_general | solution.py:63
  115.1 2.4 copy.21
  119.2 124.4 %psum.7 = f32[600]{0:T(1024)S(1)} all-reduce(f32[600]{0:T(1024)S(1)} %reduce_sum.24), channel_id=1, replica_groups=mesh['shell'=4,'sky'=8] {'sky'}, use_global_device_ids=true, to_apply=%region_6.7 | all-reduce | flops 600 | bytes 4800 | tf_op jit(solution)/shard_map/psum | solution.py:107
  (70 shorter events, 17.7 us)
Async XLA Ops:
  2.1 5.0 %collective-permute-start.1 = (f32[4,1,1,512]{3,2,1,0:T(1,128)S(1)}, f32[4,1,1,512]{3,2,1,0:T(1,128)S(1)}, u32[]{:S(2)}, u32[]{:S(2)}) collective-permute-start(f32[4,1,1,512]{3,2,1,0:T(1,128)S(1)} %pad_maximum_fusion.3), channel_id=1, source_target_pairs={{8,0},{16,8},{24,16},{9,1},{17,9},{25,17},{10,2},{18,10},{26,18},{... | collective-permute-start | bytes 24584 | tf_op jit(solution)/shard_map/ppermute | solution.py:23
  4.0 5.0 %collective-permute-start = (f32[4,1,1,512]{3,2,1,0:T(1,128)S(1)}, f32[4,1,1,512]{3,2,1,0:T(1,128)S(1)}, u32[]{:S(2)}, u32[]{:S(2)}) collective-permute-start(f32[4,1,1,512]{3,2,1,0:T(1,128)S(1)} %pad_maximum_fusion.3), channel_id=1, source_target_pairs={{0,8},{8,16},{16,24},{1,9},{9,17},{17,25},{2,10},{10,18},{18,26},{... | collective-permute-start | bytes 24584 | tf_op jit(solution)/shard_map/ppermute | solution.py:20
  9.0 6.6 %collective-permute-start.3 = (f32[4,3,1,512]{3,2,1,0:T(1,128)S(1)}, f32[4,3,1,512]{3,2,1,0:T(1,128)S(1)}, u32[]{:S(2)}, u32[]{:S(2)}) collective-permute-start(f32[4,3,1,512]{3,2,1,0:T(1,128)S(1)} %pad_maximum_fusion.2), channel_id=1, source_target_pairs={{1,0},{2,1},{3,2},{4,3},{5,4},{6,5},{7,6},{9,8},{10,9},{11,10},{12... | collective-permute-start | bytes 73736 | tf_op jit(solution)/shard_map/ppermute | solution.py:23
  10.3 6.1 %collective-permute-start.2 = (f32[4,3,1,512]{3,2,1,0:T(1,128)S(1)}, f32[4,3,1,512]{3,2,1,0:T(1,128)S(1)}, u32[]{:S(2)}, u32[]{:S(2)}) collective-permute-start(f32[4,3,1,512]{3,2,1,0:T(1,128)S(1)} %pad_maximum_fusion.2), channel_id=1, source_target_pairs={{0,1},{1,2},{2,3},{3,4},{4,5},{5,6},{6,7},{8,9},{9,10},{10,11},{11... | collective-permute-start | bytes 73736 | tf_op jit(solution)/shard_map/ppermute | solution.py:20
  16.6 227.0 %copy-start = (f32[600]{0:T(1024)S(1)}, f32[600]{0:T(1024)}, u32[]{:S(2)}) copy-start(f32[600]{0:T(1024)} %constant.397.clone) | copy-start | bytes 7204
where the time goes:
time: 245 us; the launch traced here: 244 us
  blocking collectives  124 us (51%)
  matrix products  62.4 us (25%)
  other arithmetic  38.2 us (16%)
  starting transfers between devices  10.2 us (4%)
  local copies, waits for them, and re-layouts  5.34 us (2%)
  waiting for transfers between devices  2.65 us (1%)
    psum x1, blocking collectives, local(): shell_total = lax.psum(jnp.sum(by_region, axis=0), 'sky')  124 us
    dot_general x9, matrix products, pair_block(): jnp.einsum('ijs,ijm->ism', s_weighted, mu_hot, preferred_element_type=jnp...  62.4 us
    add x9, other arithmetic, pair_block(): s_index = s_index + (squared >= edges[level]).astype(jnp.int32)  29.3 us
    ppermute x2, starting transfers between devices, padded(): lax.ppermute(lax.slice_in_dim(block, block.shape[dim] - width, None, axis...  6.95 us
    and x9, other arithmetic, pair_block(): inside = (squared >= edges[0]) & (squared < edges[S_BINS])  5.04 us
  transfers between devices with their start and end apart: 4, of which 2 were waited for; matrix products, arithmetic and copies ran while one was open for 1% of the time, Pallas kernels for 0%

commit v1 on v0

--- a/solution.py
+++ b/solution.py
@@ -104,7 +104,9 @@
 
     histogram = lax.fori_loop(0, tiles_live, add_tile, empty)
     by_region = histogram.reshape(SUBREGIONS, S_BINS * MU_BINS)
-    shell_total = lax.psum(jnp.sum(by_region, axis=0), "sky")
+    x = jnp.sum(by_region, axis=0)
+    pieces = lax.all_gather(x, "sky")
+    shell_total = jnp.sum(pieces, axis=0)
     scale = bin_scale(lax.axis_size("sky"))
     leave = (shell_total[None, :] - by_region) * scale[None, :]
     return leave.reshape(1, SUBREGIONS, S_BINS * MU_BINS)

time: 245 us -> 254 us (1.037)
  blocking collectives: 124 us -> 133 us
    all_gather x0 -> x1, blocking collectives: none -> 133 us  [local(): pieces = lax.all_gather(x, 'sky')]
    psum x1 -> x0, blocking collectives: 124 us -> none  [local(): shell_total = lax.psum(jnp.sum(by_region, axis=0), 'sky')]
where the time goes in v1:
time: 254 us; the launch traced here: 253 us
  blocking collectives  133 us (52%)
  matrix products  62.4 us (25%)
  other arithmetic  38.2 us (15%)
  starting transfers between devices  10.2 us (4%)
  local copies, waits for them, and re-layouts  5.35 us (2%)
  waiting for transfers between devices  2.65 us (1%)
    all_gather x1, blocking collectives, local(): pieces = lax.all_gather(x, 'sky')  133 us
    dot_general x9, matrix products, pair_block(): jnp.einsum('ijs,ijm->ism', s_weighted, mu_hot, preferred_element_type=jnp...  62.4 us
    add x9, other arithmetic, pair_block(): s_index = s_index + (squared >= edges[level]).astype(jnp.int32)  29.3 us
    ppermute x2, starting transfers between devices, padded(): lax.ppermute(lax.slice_in_dim(block, block.shape[dim] - width, None, axis...  6.95 us
  transfers between devices with their start and end apart: 4, of which 2 were waited for; matrix products, arithmetic and copies ran while one was open for 1% of the time, Pallas kernels for 0%

profile of v1, /device:TPU:2, one launch (start us, length us, event | category | flops | bytes accessed | tf_op | source)
XLA Modules:
  0.0 252.8 jit_solution(6490611206848121961)
XLA Ops:
  4.0 2.4 collective-permute-start
  10.3 4.5 %collective-permute-start.2 = (f32[4,3,1,512]{3,2,1,0:T(1,128)S(1)}, f32[4,3,1,512]{3,2,1,0:T(1,128)S(1)}, u32[]{:S(2)}, u32[]{:S(2)}) collective-permute-start(f32[4,3,1,512]{3,2,1,0:T(1,128)S(1)} %pad_maximum_fusion.2), channel_id=1, source_target_pairs={{0,1},{1,2},{2,3},{3,4},{4,5},{5,6},{6,7},{8,9},{9,10},{10,11},{11... | collective-permute-start | bytes 73736 | tf_op jit(solution)/shard_map/ppermute | solution.py:20
  16.6 101.9 %while.36 = (s32[]{:T(128)}, f32[8,30,20]{0,2,1:T(8,128)S(1)}, s32[]{:T(128)}, s32[3,512]{1,0:T(4,128)S(1)}, f32[512]{0:T(512)S(1)}, /*index=5*/s32[3,4608]{1,0:...) while((s32[]{:T(128)}, f32[8,30,20]{0,2,1:T(8,128)S(1)}, ...), condition=%wide.region_4.5_spmd.clone, body=%wide.region_0.4_spmd.clone.sunk | while | flops 199642880 | bytes 5579304 | solution.py:105
  16.6 98.5 %while.37 = (s32[]{:T(128)}, f32[256,30,20]{1,2,0:T(8,128)}, s32[3,256]{1,0:T(4,128)S(1)}, s32[3,4608]{1,0:T(4,128)S(1)}, bf16[4608]{0:T(1024)(128)(2,1)S(1)}, /...) while((s32[]{:T(128)}, f32[256,30,20]{1,2,0:T(8,128)}, ...), condition=%wide.region_2.2_spmd.clone, body=%wide.region_1.1_spmd.clone.sunk | while | flops 197177344 | bytes 3628245 | solution.py:95
  16.8 3.3 %convert_add_fusion.3 = (s32[256,512]{1,0:T(8,128)S(1)}, s32[256,512]{1,0:T(8,128)S(1)}) fusion(s32[512]{0:T(512)S(1)} %bitcast.35, s32[256]{0:T(256)S(1)} %bitcast.39, s32[512]{0:T(512)S(1)} %bitcast.31, s32[256]{0:T(256)S(1)} %bitcast.37, s32[512]{0:T(512)S(1)} %bitcast.33, s32[256]{0:T(256)S(1)} %bitcast.41), kind=kLoop, calls=%fused_computation.31.clone.1 | loop fusion | flops 22937600 | bytes 1057792 | tf_op jit(solution)/shard_map/while/body/while/body/eval_jaxpr/add | solution.py:51
  20.7 5.7 %select_add_fusion.2 = f32[256,30,20]{1,2,0:T(8,128)} fusion(f32[256,30,20]{1,2,0:T(8,128)} %get-tuple-element.400, s32[256,512]{1,0:T(8,128)S(1)} %get-tuple-element.386, bf16[512]{0:T(512)(128)(2,1)S(1)} %dynamic_slice.36, s32[256,512]{1,0:T(8,128)S(1)} %get-tuple-element.387, pred[256,512]{1,0:T(8,128)(4,1)S(1)} %compare_and_fusion.2, ...), kind=kOutput, calls=%fused_computation.11.clone.1 | convolution fusion | flops 172011520 | bytes 2409473 | tf_op jit(solution)/shard_map/while/body/while/body/eval_jaxpr/ijs,ijm->ism/dot_general | solution.py:63
  26.5 3.3 %convert_add_fusion.3 = (s32[256,512]{1,0:T(8,128)S(1)}, s32[256,512]{1,0:T(8,128)S(1)}) fusion(s32[512]{0:T(512)S(1)} %bitcast.35, s32[256]{0:T(256)S(1)} %bitcast.39, s32[512]{0:T(512)S(1)} %bitcast.31, s32[256]{0:T(256)S(1)} %bitcast.37, s32[512]{0:T(512)S(1)} %bitcast.33, s32[256]{0:T(256)S(1)} %bitcast.41), kind=kLoop, calls=%fused_computation.31.clone.1 | loop fusion | flops 22937600 | bytes 1057792 | tf_op jit(solution)/shard_map/while/body/while/body/eval_jaxpr/add | solution.py:51
  30.4 7.1 %select_add_fusion.2 = f32[256,30,20]{1,2,0:T(8,128)} fusion(f32[256,30,20]{1,2,0:T(8,128)} %get-tuple-element.400, s32[256,512]{1,0:T(8,128)S(1)} %get-tuple-element.386, bf16[512]{0:T(512)(128)(2,1)S(1)} %dynamic_slice.36, s32[256,512]{1,0:T(8,128)S(1)} %get-tuple-element.387, pred[256,512]{1,0:T(8,128)(4,1)S(1)} %compare_and_fusion.2, ...), kind=kOutput, calls=%fused_computation.11.clone.1 | convolution fusion | flops 172011520 | bytes 2409473 | tf_op jit(solution)/shard_map/while/body/while/body/eval_jaxpr/ijs,ijm->ism/dot_general | solution.py:63
  37.6 3.3 %convert_add_fusion.3 = (s32[256,512]{1,0:T(8,128)S(1)}, s32[256,512]{1,0:T(8,128)S(1)}) fusion(s32[512]{0:T(512)S(1)} %bitcast.35, s32[256]{0:T(256)S(1)} %bitcast.39, s32[512]{0:T(512)S(1)} %bitcast.31, s32[256]{0:T(256)S(1)} %bitcast.37, s32[512]{0:T(512)S(1)} %bitcast.33, s32[256]{0:T(256)S(1)} %bitcast.41), kind=kLoop, calls=%fused_computation.31.clone.1 | loop fusion | flops 22937600 | bytes 1057792 | tf_op jit(solution)/shard_map/while/body/while/body/eval_jaxpr/add | solution.py:51
  41.5 7.1 %select_add_fusion.2 = f32[256,30,20]{1,2,0:T(8,128)} fusion(f32[256,30,20]{1,2,0:T(8,128)} %get-tuple-element.400, s32[256,512]{1,0:T(8,128)S(1)} %get-tuple-element.386, bf16[512]{0:T(512)(128)(2,1)S(1)} %dynamic_slice.36, s32[256,512]{1,0:T(8,128)S(1)} %get-tuple-element.387, pred[256,512]{1,0:T(8,128)(4,1)S(1)} %compare_and_fusion.2, ...), kind=kOutput, calls=%fused_computation.11.clone.1 | convolution fusion | flops 172011520 | bytes 2409473 | tf_op jit(solution)/shard_map/while/body/while/body/eval_jaxpr/ijs,ijm->ism/dot_general | solution.py:63
  48.7 3.3 %convert_add_fusion.3 = (s32[256,512]{1,0:T(8,128)S(1)}, s32[256,512]{1,0:T(8,128)S(1)}) fusion(s32[512]{0:T(512)S(1)} %bitcast.35, s32[256]{0:T(256)S(1)} %bitcast.39, s32[512]{0:T(512)S(1)} %bitcast.31, s32[256]{0:T(256)S(1)} %bitcast.37, s32[512]{0:T(512)S(1)} %bitcast.33, s32[256]{0:T(256)S(1)} %bitcast.41), kind=kLoop, calls=%fused_computation.31.clone.1 | loop fusion | flops 22937600 | bytes 1057792 | tf_op jit(solution)/shard_map/while/body/while/body/eval_jaxpr/add | solution.py:51
  52.6 7.1 %select_add_fusion.2 = f32[256,30,20]{1,2,0:T(8,128)} fusion(f32[256,30,20]{1,2,0:T(8,128)} %get-tuple-element.400, s32[256,512]{1,0:T(8,128)S(1)} %get-tuple-element.386, bf16[512]{0:T(512)(128)(2,1)S(1)} %dynamic_slice.36, s32[256,512]{1,0:T(8,128)S(1)} %get-tuple-element.387, pred[256,512]{1,0:T(8,128)(4,1)S(1)} %compare_and_fusion.2, ...), kind=kOutput, calls=%fused_computation.11.clone.1 | convolution fusion | flops 172011520 | bytes 2409473 | tf_op jit(solution)/shard_map/while/body/while/body/eval_jaxpr/ijs,ijm->ism/dot_general | solution.py:63
  59.8 3.3 %convert_add_fusion.3 = (s32[256,512]{1,0:T(8,128)S(1)}, s32[256,512]{1,0:T(8,128)S(1)}) fusion(s32[512]{0:T(512)S(1)} %bitcast.35, s32[256]{0:T(256)S(1)} %bitcast.39, s32[512]{0:T(512)S(1)} %bitcast.31, s32[256]{0:T(256)S(1)} %bitcast.37, s32[512]{0:T(512)S(1)} %bitcast.33, s32[256]{0:T(256)S(1)} %bitcast.41), kind=kLoop, calls=%fused_computation.31.clone.1 | loop fusion | flops 22937600 | bytes 1057792 | tf_op jit(solution)/shard_map/while/body/while/body/eval_jaxpr/add | solution.py:51
  63.7 7.1 %select_add_fusion.2 = f32[256,30,20]{1,2,0:T(8,128)} fusion(f32[256,30,20]{1,2,0:T(8,128)} %get-tuple-element.400, s32[256,512]{1,0:T(8,128)S(1)} %get-tuple-element.386, bf16[512]{0:T(512)(128)(2,1)S(1)} %dynamic_slice.36, s32[256,512]{1,0:T(8,128)S(1)} %get-tuple-element.387, pred[256,512]{1,0:T(8,128)(4,1)S(1)} %compare_and_fusion.2, ...), kind=kOutput, calls=%fused_computation.11.clone.1 | convolution fusion | flops 172011520 | bytes 2409473 | tf_op jit(solution)/shard_map/while/body/while/body/eval_jaxpr/ijs,ijm->ism/dot_general | solution.py:63
  70.8 3.3 %convert_add_fusion.3 = (s32[256,512]{1,0:T(8,128)S(1)}, s32[256,512]{1,0:T(8,128)S(1)}) fusion(s32[512]{0:T(512)S(1)} %bitcast.35, s32[256]{0:T(256)S(1)} %bitcast.39, s32[512]{0:T(512)S(1)} %bitcast.31, s32[256]{0:T(256)S(1)} %bitcast.37, s32[512]{0:T(512)S(1)} %bitcast.33, s32[256]{0:T(256)S(1)} %bitcast.41), kind=kLoop, calls=%fused_computation.31.clone.1 | loop fusion | flops 22937600 | bytes 1057792 | tf_op jit(solution)/shard_map/while/body/while/body/eval_jaxpr/add | solution.py:51
  74.8 7.1 %select_add_fusion.2 = f32[256,30,20]{1,2,0:T(8,128)} fusion(f32[256,30,20]{1,2,0:T(8,128)} %get-tuple-element.400, s32[256,512]{1,0:T(8,128)S(1)} %get-tuple-element.386, bf16[512]{0:T(512)(128)(2,1)S(1)} %dynamic_slice.36, s32[256,512]{1,0:T(8,128)S(1)} %get-tuple-element.387, pred[256,512]{1,0:T(8,128)(4,1)S(1)} %compare_and_fusion.2, ...), kind=kOutput, calls=%fused_computation.11.clone.1 | convolution fusion | flops 172011520 | bytes 2409473 | tf_op jit(solution)/shard_map/while/body/while/body/eval_jaxpr/ijs,ijm->ism/dot_general | solution.py:63
  81.9 3.3 %convert_add_fusion.3 = (s32[256,512]{1,0:T(8,128)S(1)}, s32[256,512]{1,0:T(8,128)S(1)}) fusion(s32[512]{0:T(512)S(1)} %bitcast.35, s32[256]{0:T(256)S(1)} %bitcast.39, s32[512]{0:T(512)S(1)} %bitcast.31, s32[256]{0:T(256)S(1)} %bitcast.37, s32[512]{0:T(512)S(1)} %bitcast.33, s32[256]{0:T(256)S(1)} %bitcast.41), kind=kLoop, calls=%fused_computation.31.clone.1 | loop fusion | flops 22937600 | bytes 1057792 | tf_op jit(solution)/shard_map/while/body/while/body/eval_jaxpr/add | solution.py:51
  85.9 7.1 %select_add_fusion.2 = f32[256,30,20]{1,2,0:T(8,128)} fusion(f32[256,30,20]{1,2,0:T(8,128)} %get-tuple-element.400, s32[256,512]{1,0:T(8,128)S(1)} %get-tuple-element.386, bf16[512]{0:T(512)(128)(2,1)S(1)} %dynamic_slice.36, s32[256,512]{1,0:T(8,128)S(1)} %get-tuple-element.387, pred[256,512]{1,0:T(8,128)(4,1)S(1)} %compare_and_fusion.2, ...), kind=kOutput, calls=%fused_computation.11.clone.1 | convolution fusion | flops 172011520 | bytes 2409473 | tf_op jit(solution)/shard_map/while/body/while/body/eval_jaxpr/ijs,ijm->ism/dot_general | solution.py:63
  93.0 3.3 %convert_add_fusion.3 = (s32[256,512]{1,0:T(8,128)S(1)}, s32[256,512]{1,0:T(8,128)S(1)}) fusion(s32[512]{0:T(512)S(1)} %bitcast.35, s32[256]{0:T(256)S(1)} %bitcast.39, s32[512]{0:T(512)S(1)} %bitcast.31, s32[256]{0:T(256)S(1)} %bitcast.37, s32[512]{0:T(512)S(1)} %bitcast.33, s32[256]{0:T(256)S(1)} %bitcast.41), kind=kLoop, calls=%fused_computation.31.clone.1 | loop fusion | flops 22937600 | bytes 1057792 | tf_op jit(solution)/shard_map/while/body/while/body/eval_jaxpr/add | solution.py:51
  96.9 7.1 %select_add_fusion.2 = f32[256,30,20]{1,2,0:T(8,128)} fusion(f32[256,30,20]{1,2,0:T(8,128)} %get-tuple-element.400, s32[256,512]{1,0:T(8,128)S(1)} %get-tuple-element.386, bf16[512]{0:T(512)(128)(2,1)S(1)} %dynamic_slice.36, s32[256,512]{1,0:T(8,128)S(1)} %get-tuple-element.387, pred[256,512]{1,0:T(8,128)(4,1)S(1)} %compare_and_fusion.2, ...), kind=kOutput, calls=%fused_computation.11.clone.1 | convolution fusion | flops 172011520 | bytes 2409473 | tf_op jit(solution)/shard_map/while/body/while/body/eval_jaxpr/ijs,ijm->ism/dot_general | solution.py:63
  104.1 3.3 %convert_add_fusion.3 = (s32[256,512]{1,0:T(8,128)S(1)}, s32[256,512]{1,0:T(8,128)S(1)}) fusion(s32[512]{0:T(512)S(1)} %bitcast.35, s32[256]{0:T(256)S(1)} %bitcast.39, s32[512]{0:T(512)S(1)} %bitcast.31, s32[256]{0:T(256)S(1)} %bitcast.37, s32[512]{0:T(512)S(1)} %bitcast.33, s32[256]{0:T(256)S(1)} %bitcast.41), kind=kLoop, calls=%fused_computation.31.clone.1 | loop fusion | flops 22937600 | bytes 1057792 | tf_op jit(solution)/shard_map/while/body/while/body/eval_jaxpr/add | solution.py:51
  108.0 7.1 %select_add_fusion.2 = f32[256,30,20]{1,2,0:T(8,128)} fusion(f32[256,30,20]{1,2,0:T(8,128)} %get-tuple-element.400, s32[256,512]{1,0:T(8,128)S(1)} %get-tuple-element.386, bf16[512]{0:T(512)(128)(2,1)S(1)} %dynamic_slice.36, s32[256,512]{1,0:T(8,128)S(1)} %get-tuple-element.387, pred[256,512]{1,0:T(8,128)(4,1)S(1)} %compare_and_fusion.2, ...), kind=kOutput, calls=%fused_computation.11.clone.1 | convolution fusion | flops 172011520 | bytes 2409473 | tf_op jit(solution)/shard_map/while/body/while/body/eval_jaxpr/ijs,ijm->ism/dot_general | solution.py:63
  115.1 2.4 copy.21
  119.2 133.0 %all-gather = f32[8,1,600]{2,1,0:T(1,128)S(1)} all-gather(f32[1,1,600]{2,1,0:T(1,128)S(1)} %reshape.666), channel_id=1, replica_groups=mesh['shell'=4,'sky'=8] {'sky'}, dimensions={0}, use_global_device_ids=true | all-gather | bytes 21600 | tf_op jit(solution)/shard_map/all_gather | solution.py:108
  (71 shorter events, 17.7 us)
Async XLA Ops:
  2.1 5.0 %collective-permute-start.1 = (f32[4,1,1,512]{3,2,1,0:T(1,128)S(1)}, f32[4,1,1,512]{3,2,1,0:T(1,128)S(1)}, u32[]{:S(2)}, u32[]{:S(2)}) collective-permute-start(f32[4,1,1,512]{3,2,1,0:T(1,128)S(1)} %pad_maximum_fusion.3), channel_id=1, source_target_pairs={{8,0},{16,8},{24,16},{9,1},{17,9},{25,17},{10,2},{18,10},{26,18},{... | collective-permute-start | bytes 24584 | tf_op jit(solution)/shard_map/ppermute | solution.py:23
  4.0 5.0 %collective-permute-start = (f32[4,1,1,512]{3,2,1,0:T(1,128)S(1)}, f32[4,1,1,512]{3,2,1,0:T(1,128)S(1)}, u32[]{:S(2)}, u32[]{:S(2)}) collective-permute-start(f32[4,1,1,512]{3,2,1,0:T(1,128)S(1)} %pad_maximum_fusion.3), channel_id=1, source_target_pairs={{0,8},{8,16},{16,24},{1,9},{9,17},{17,25},{2,10},{10,18},{18,26},{... | collective-permute-start | bytes 24584 | tf_op jit(solution)/shard_map/ppermute | solution.py:20
  9.0 6.6 %collective-permute-start.3 = (f32[4,3,1,512]{3,2,1,0:T(1,128)S(1)}, f32[4,3,1,512]{3,2,1,0:T(1,128)S(1)}, u32[]{:S(2)}, u32[]{:S(2)}) collective-permute-start(f32[4,3,1,512]{3,2,1,0:T(1,128)S(1)} %pad_maximum_fusion.2), channel_id=1, source_target_pairs={{1,0},{2,1},{3,2},{4,3},{5,4},{6,5},{7,6},{9,8},{10,9},{11,10},{12... | collective-permute-start | bytes 73736 | tf_op jit(solution)/shard_map/ppermute | solution.py:23
  10.3 6.1 %collective-permute-start.2 = (f32[4,3,1,512]{3,2,1,0:T(1,128)S(1)}, f32[4,3,1,512]{3,2,1,0:T(1,128)S(1)}, u32[]{:S(2)}, u32[]{:S(2)}) collective-permute-start(f32[4,3,1,512]{3,2,1,0:T(1,128)S(1)} %pad_maximum_fusion.2), channel_id=1, source_target_pairs={{0,1},{1,2},{2,3},{3,4},{4,5},{5,6},{6,7},{8,9},{9,10},{10,11},{11... | collective-permute-start | bytes 73736 | tf_op jit(solution)/shard_map/ppermute | solution.py:20
  16.6 235.6 %copy-start = (f32[600]{0:T(1024)S(1)}, f32[600]{0:T(1024)}, u32[]{:S(2)}) copy-start(f32[600]{0:T(1024)} %constant.397.clone) | copy-start | bytes 7204
